TPU v7x, 32 devices: a whole 2x2x4 slice. The times are simulated.
32 devices in a mesh: dp: 8 (over y, x, core), seq: 4 (over z).
Axes of the slice: x: 2, y: 2, z: 4, core: 2. Of those that a mesh axis runs over, the one named last changes fastest.
Arguments:
- inputs: bfloat16 [24, 1024, 768], P('dp', 'seq'), may hold values from -6 to 6
- segment_ids: int32 [24, 1024], P('dp', 'seq'), may hold values from 0 to 3, never falling along the last dimension, each value on 1 to 512 neighbouring positions
- norm1_gain: bfloat16 [768], P('dp'), may hold values from 0.5 to 1.5
- norm1_shift: bfloat16 [768], P('dp'), may hold values from -1.5 to 1.5
- query_weight: bfloat16 [768, 768], P('dp'), may hold values from -0.4375 to 0.4375
- query_bias: bfloat16 [768], P('dp'), may hold values from -2.5 to 2.5
- key_weight: bfloat16 [768, 768], P('dp'), may hold values from -0.21875 to 0.21875
- value_weight: bfloat16 [768, 768], P('dp'), may hold values from -0.21875 to 0.21875
- value_bias: bfloat16 [768], P('dp'), may hold values from -1.5 to 1.5
- out_weight: bfloat16 [768, 768], P('dp'), may hold values from -0.625 to 0.625
- out_bias: bfloat16 [768], P('dp'), may hold values from -1.5 to 1.5
- norm2_gain: bfloat16 [768], P('dp'), may hold values from 0.5 to 1.5
- norm2_shift: bfloat16 [768], P('dp'), may hold values from -1.5 to 1.5
- fc1_weight: bfloat16 [768, 3072], P('dp'), may hold values from -0.21875 to 0.21875
- fc1_bias: bfloat16 [3072], P('dp'), may hold values from -1.5 to 1.5
- fc2_weight: bfloat16 [3072, 768], P('dp'), may hold values from -0.15625 to 0.15625
- fc2_bias: bfloat16 [768], P('dp'), may hold values from -1.5 to 1.5
- grad_output: bfloat16 [24, 1024, 768], P('dp', 'seq'), may hold values from -6 to 6
Outputs:
- output: bfloat16 [24, 1024, 768], P('dp', 'seq')
- grad_inputs: bfloat16 [24, 1024, 768], P('dp', 'seq')
- grad_norm1_gain: float32 [768], P('dp')
- grad_norm1_shift: float32 [768], P('dp')
- grad_query_weight: float32 [768, 768], P('dp')
- grad_query_bias: float32 [768], P('dp')
- grad_key_weight: float32 [768, 768], P('dp')
- grad_value_weight: float32 [768, 768], P('dp')
- grad_value_bias: float32 [768], P('dp')
- grad_out_weight: float32 [768, 768], P('dp')
- grad_out_bias: float32 [768], P('dp')
- grad_norm2_gain: float32 [768], P('dp')
- grad_norm2_shift: float32 [768], P('dp')
- grad_fc1_weight: float32 [768, 3072], P('dp')
- grad_fc1_bias: float32 [3072], P('dp')
- grad_fc2_weight: float32 [3072, 768], P('dp')
- grad_fc2_bias: float32 [768], P('dp')
Inputs may be any that keep to these rules, and one draw needn't show every extreme that they name: `segment_ids`: within each sequence, segment numbers never fall along the positions; each segment is a run of 1 to 512 positions.
All inputs are finite; a program needn't handle non-finite values.
Results may differ from a plain program's by a relative error of at most 0.017.
Values may be sent and summed in bfloat16 or wider, within the bound.
No kernel may reach another device: no remote copies, remote signals or barrier semaphores. Data moves between devices by JAX's collectives and lax.ppermute only.
A program may use at most 192 MiB of HBM per device.

v0:
```python
import jax
import jax.numpy as jnp
from jax import lax
from jax.sharding import PartitionSpec as P

HD = 64
EPSILON = 1e-05


def layer_norm(values, gain, shift):
    center = values - jnp.mean(values, axis=-1, keepdims=True)
    inverse = lax.rsqrt(jnp.mean(center * center, axis=-1, keepdims=True) + EPSILON)
    normed = center * inverse
    return (normed * gain + shift, normed, inverse)


def norm_back(grad, normed, inverse, gain):
    scaled = grad * gain
    return inverse * (
        scaled
        - jnp.mean(scaled, axis=-1, keepdims=True)
        - normed * jnp.mean(scaled * normed, axis=-1, keepdims=True)
    )


def gelu_slope(pre_act):
    return (
        0.5 * (1.0 + lax.erf(pre_act * 0.7071067811865476))
        + pre_act * jnp.exp(-0.5 * pre_act * pre_act) * 0.3989422804014327
    )


def cross_rows(left, right):
    return lax.dot_general(
        left, right, (((0,), (0,)), ((), ())), preferred_element_type=jnp.float32
    )


def times_transpose(left, right):
    return lax.dot_general(
        left, right, (((1,), (1,)), ((), ())), preferred_element_type=jnp.float32
    )


def to_pairs(array, heads_here):
    seqs_here, positions, _ = array.shape
    shaped = array.reshape(seqs_here, positions, heads_here, HD).transpose(0, 2, 1, 3)
    return shaped.reshape(seqs_here * heads_here, positions, HD)


def from_pairs(array, seqs_here, heads_here):
    positions = array.shape[1]
    shaped = array.reshape(seqs_here, heads_here, positions, HD).transpose(0, 2, 1, 3)
    return shaped.reshape(seqs_here, positions, heads_here * HD)


def masked_scores(query_pair, key_pair, segment_row):
    scores = jnp.einsum(
        "qd,kd->qk", query_pair, key_pair, preferred_element_type=jnp.float32
    ) * HD ** (-0.5)
    same_segment = segment_row[:, None] == segment_row[None, :]
    return jnp.where(same_segment, scores, -1e30)


def attend_forward(packed):
    query_pair, key_pair, value_pair, segment_row = packed
    scores = masked_scores(query_pair, key_pair, segment_row)
    highest = jnp.max(scores, axis=-1, keepdims=True)
    expon = jnp.exp(scores - highest)
    totals = jnp.sum(expon, axis=-1, keepdims=True)
    probs = (expon / totals).astype(jnp.bfloat16)
    result = jnp.dot(probs, value_pair, preferred_element_type=jnp.float32).astype(jnp.bfloat16)
    return (result, (highest + jnp.log(totals))[:, 0])


def attend_backward(packed):
    query_pair, key_pair, value_pair, segment_row, logsum, grad_pair = packed
    scores = masked_scores(query_pair, key_pair, segment_row)
    probs = jnp.exp(scores - logsum[:, None])
    grad_probs = jnp.einsum("qd,kd->qk", grad_pair, value_pair, preferred_element_type=jnp.float32)
    delta = jnp.sum(probs * grad_probs, axis=-1, keepdims=True)
    grad_scores = (probs * (grad_probs - delta)).astype(jnp.bfloat16)
    factor = HD ** (-0.5)
    grad_query = (
        jnp.einsum("qk,kd->qd", grad_scores, key_pair, preferred_element_type=jnp.float32) * factor
    ).astype(jnp.bfloat16)
    grad_key = (
        jnp.einsum("qk,qd->kd", grad_scores, query_pair, preferred_element_type=jnp.float32)
        * factor
    ).astype(jnp.bfloat16)
    grad_value = jnp.einsum(
        "qk,qd->kd", probs.astype(jnp.bfloat16), grad_pair, preferred_element_type=jnp.float32
    ).astype(jnp.bfloat16)
    return (grad_query, grad_key, grad_value)


def column_sum(array):
    return jnp.sum(array.astype(jnp.float32), axis=0)


def per_device(
    inputs,
    segment_ids,
    norm1_gain,
    norm1_shift,
    query_weight,
    query_bias,
    key_weight,
    value_weight,
    value_bias,
    out_weight,
    out_bias,
    norm2_gain,
    norm2_shift,
    fc1_weight,
    fc1_bias,
    fc2_weight,
    fc2_bias,
    grad_output,
):
    seqs_here, positions, model_width = inputs.shape
    token_rows = seqs_here * positions
    (
        first_gain,
        first_shift,
        w_query,
        b_query,
        w_key,
        w_value,
        b_value,
        w_out,
        b_out,
        second_gain,
        second_shift,
        w_up,
        b_up,
        w_down,
        b_down,
    ) = (
        lax.all_gather(norm1_gain, "dp", axis=0, tiled=True),
        lax.all_gather(norm1_shift, "dp", axis=0, tiled=True),
        lax.all_gather(query_weight, "dp", axis=0, tiled=True),
        lax.all_gather(query_bias, "dp", axis=0, tiled=True),
        lax.all_gather(key_weight, "dp", axis=0, tiled=True),
        lax.all_gather(value_weight, "dp", axis=0, tiled=True),
        lax.all_gather(value_bias, "dp", axis=0, tiled=True),
        lax.all_gather(out_weight, "dp", axis=0, tiled=True),
        lax.all_gather(out_bias, "dp", axis=0, tiled=True),
        lax.all_gather(norm2_gain, "dp", axis=0, tiled=True),
        lax.all_gather(norm2_shift, "dp", axis=0, tiled=True),
        lax.all_gather(fc1_weight, "dp", axis=0, tiled=True),
        lax.all_gather(fc1_bias, "dp", axis=0, tiled=True),
        lax.all_gather(fc2_weight, "dp", axis=0, tiled=True),
        lax.all_gather(fc2_bias, "dp", axis=0, tiled=True),
    )
    full_segments = lax.all_gather(segment_ids, "seq", axis=1, tiled=True)
    flat_in = inputs.reshape(token_rows, model_width).astype(jnp.float32)
    normed_one, unit_one, inverse_one = layer_norm(
        flat_in, first_gain.astype(jnp.float32), first_shift.astype(jnp.float32)
    )
    act_one = normed_one.astype(jnp.bfloat16)
    query_tok = (
        jnp.dot(act_one, w_query, preferred_element_type=jnp.float32) + b_query.astype(jnp.float32)
    ).astype(jnp.bfloat16)
    key_tok = jnp.dot(act_one, w_key, preferred_element_type=jnp.float32).astype(jnp.bfloat16)
    value_tok = (
        jnp.dot(act_one, w_value, preferred_element_type=jnp.float32) + b_value.astype(jnp.float32)
    ).astype(jnp.bfloat16)
    query_heads, key_heads, value_heads = (
        lax.all_to_all(
            query_tok.reshape(seqs_here, positions, model_width),
            "seq",
            split_axis=2,
            concat_axis=1,
            tiled=True,
        ),
        lax.all_to_all(
            key_tok.reshape(seqs_here, positions, model_width),
            "seq",
            split_axis=2,
            concat_axis=1,
            tiled=True,
        ),
        lax.all_to_all(
            value_tok.reshape(seqs_here, positions, model_width),
            "seq",
            split_axis=2,
            concat_axis=1,
            tiled=True,
        ),
    )
    heads_here = query_heads.shape[2] // HD
    query_pairs = to_pairs(query_heads, heads_here)
    key_pairs = to_pairs(key_heads, heads_here)
    value_pairs = to_pairs(value_heads, heads_here)
    segment_pairs = jnp.repeat(full_segments, heads_here, axis=0)
    attn_pairs, logsum = lax.map(
        attend_forward, (query_pairs, key_pairs, value_pairs, segment_pairs)
    )
    attn_heads = from_pairs(attn_pairs, seqs_here, heads_here)
    attn_tok = lax.all_to_all(attn_heads, "seq", split_axis=1, concat_axis=2, tiled=True).reshape(
        token_rows, model_width
    )
    middle = (
        flat_in
        + jnp.dot(attn_tok, w_out, preferred_element_type=jnp.float32)
        + b_out.astype(jnp.float32)
    )
    normed_two, unit_two, inverse_two = layer_norm(
        middle, second_gain.astype(jnp.float32), second_shift.astype(jnp.float32)
    )
    act_two = normed_two.astype(jnp.bfloat16)
    pre_act = jnp.dot(act_two, w_up, preferred_element_type=jnp.float32) + b_up.astype(jnp.float32)
    hidden = jax.nn.gelu(pre_act, approximate=False).astype(jnp.bfloat16)
    result = (
        middle
        + jnp.dot(hidden, w_down, preferred_element_type=jnp.float32)
        + b_down.astype(jnp.float32)
    )
    output = result.astype(jnp.bfloat16).reshape(seqs_here, positions, model_width)
    first_gain_b, w_query_b, w_key_b, w_value_b, w_out_b, second_gain_b, w_up_b, w_down_b = (
        lax.all_gather(norm1_gain, "dp", axis=0, tiled=True),
        lax.all_gather(query_weight, "dp", axis=0, tiled=True),
        lax.all_gather(key_weight, "dp", axis=0, tiled=True),
        lax.all_gather(value_weight, "dp", axis=0, tiled=True),
        lax.all_gather(out_weight, "dp", axis=0, tiled=True),
        lax.all_gather(norm2_gain, "dp", axis=0, tiled=True),
        lax.all_gather(fc1_weight, "dp", axis=0, tiled=True),
        lax.all_gather(fc2_weight, "dp", axis=0, tiled=True),
    )
    grad_down = grad_output.reshape(token_rows, model_width)
    d_b_down = column_sum(grad_down)
    d_w_down = cross_rows(hidden, grad_down)
    grad_hidden = times_transpose(grad_down, w_down_b)
    grad_pre = (grad_hidden * gelu_slope(pre_act)).astype(jnp.bfloat16)
    d_b_up = column_sum(grad_pre)
    d_w_up = cross_rows(act_two, grad_pre)
    grad_two = times_transpose(grad_pre, w_up_b)
    d_second_gain = jnp.sum(grad_two * unit_two, axis=0)
    d_second_shift = jnp.sum(grad_two, axis=0)
    grad_middle = grad_down.astype(jnp.float32) + norm_back(
        grad_two, unit_two, inverse_two, second_gain_b.astype(jnp.float32)
    )
    grad_branch = grad_middle.astype(jnp.bfloat16)
    d_b_out = column_sum(grad_branch)
    d_w_out = cross_rows(attn_tok, grad_branch)
    grad_attn = (
        times_transpose(grad_branch, w_out_b)
        .astype(jnp.bfloat16)
        .reshape(seqs_here, positions, model_width)
    )
    grad_attn_heads = lax.all_to_all(grad_attn, "seq", split_axis=2, concat_axis=1, tiled=True)
    grad_query_pairs, grad_key_pairs, grad_value_pairs = lax.map(
        attend_backward,
        (
            query_pairs,
            key_pairs,
            value_pairs,
            segment_pairs,
            logsum,
            to_pairs(grad_attn_heads, heads_here),
        ),
    )
    grad_query_tok, grad_key_tok, grad_value_tok = (
        lax.all_to_all(
            from_pairs(grad_query_pairs, seqs_here, heads_here),
            "seq",
            split_axis=1,
            concat_axis=2,
            tiled=True,
        ),
        lax.all_to_all(
            from_pairs(grad_key_pairs, seqs_here, heads_here),
            "seq",
            split_axis=1,
            concat_axis=2,
            tiled=True,
        ),
        lax.all_to_all(
            from_pairs(grad_value_pairs, seqs_here, heads_here),
            "seq",
            split_axis=1,
            concat_axis=2,
            tiled=True,
        ),
    )
    grad_query_tok = grad_query_tok.reshape(token_rows, model_width)
    grad_key_tok = grad_key_tok.reshape(token_rows, model_width)
    grad_value_tok = grad_value_tok.reshape(token_rows, model_width)
    d_b_query = column_sum(grad_query_tok)
    d_b_value = column_sum(grad_value_tok)
    d_w_query = cross_rows(act_one, grad_query_tok)
    d_w_key = cross_rows(act_one, grad_key_tok)
    d_w_value = cross_rows(act_one, grad_value_tok)
    grad_one = (
        times_transpose(grad_query_tok, w_query_b)
        + times_transpose(grad_key_tok, w_key_b)
        + times_transpose(grad_value_tok, w_value_b)
    )
    d_first_gain = jnp.sum(grad_one * unit_one, axis=0)
    d_first_shift = jnp.sum(grad_one, axis=0)
    grad_inputs = grad_middle + norm_back(
        grad_one, unit_one, inverse_one, first_gain_b.astype(jnp.float32)
    )
    grad_inputs = grad_inputs.astype(jnp.bfloat16).reshape(seqs_here, positions, model_width)
    (
        part_first_gain,
        part_first_shift,
        part_w_query,
        part_b_query,
        part_w_key,
        part_w_value,
        part_b_value,
        part_w_out,
        part_b_out,
        part_second_gain,
        part_second_shift,
        part_w_up,
        part_b_up,
        part_w_down,
        part_b_down,
    ) = (
        lax.psum_scatter(d_first_gain, "dp", scatter_dimension=0, tiled=True),
        lax.psum_scatter(d_first_shift, "dp", scatter_dimension=0, tiled=True),
        lax.psum_scatter(d_w_query, "dp", scatter_dimension=0, tiled=True),
        lax.psum_scatter(d_b_query, "dp", scatter_dimension=0, tiled=True),
        lax.psum_scatter(d_w_key, "dp", scatter_dimension=0, tiled=True),
        lax.psum_scatter(d_w_value, "dp", scatter_dimension=0, tiled=True),
        lax.psum_scatter(d_b_value, "dp", scatter_dimension=0, tiled=True),
        lax.psum_scatter(d_w_out, "dp", scatter_dimension=0, tiled=True),
        lax.psum_scatter(d_b_out, "dp", scatter_dimension=0, tiled=True),
        lax.psum_scatter(d_second_gain, "dp", scatter_dimension=0, tiled=True),
        lax.psum_scatter(d_second_shift, "dp", scatter_dimension=0, tiled=True),
        lax.psum_scatter(d_w_up, "dp", scatter_dimension=0, tiled=True),
        lax.psum_scatter(d_b_up, "dp", scatter_dimension=0, tiled=True),
        lax.psum_scatter(d_w_down, "dp", scatter_dimension=0, tiled=True),
        lax.psum_scatter(d_b_down, "dp", scatter_dimension=0, tiled=True),
    )
    (
        shard_first_gain,
        shard_first_shift,
        shard_w_query,
        shard_b_query,
        shard_w_key,
        shard_w_value,
        shard_b_value,
        shard_w_out,
        shard_b_out,
        shard_second_gain,
        shard_second_shift,
        shard_w_up,
        shard_b_up,
        shard_w_down,
        shard_b_down,
    ) = (
        lax.psum(part_first_gain.astype(jnp.bfloat16), "seq").astype(jnp.float32),
        lax.psum(part_first_shift.astype(jnp.bfloat16), "seq").astype(jnp.float32),
        lax.psum(part_w_query.astype(jnp.bfloat16), "seq").astype(jnp.float32),
        lax.psum(part_b_query.astype(jnp.bfloat16), "seq").astype(jnp.float32),
        lax.psum(part_w_key.astype(jnp.bfloat16), "seq").astype(jnp.float32),
        lax.psum(part_w_value.astype(jnp.bfloat16), "seq").astype(jnp.float32),
        lax.psum(part_b_value.astype(jnp.bfloat16), "seq").astype(jnp.float32),
        lax.psum(part_w_out.astype(jnp.bfloat16), "seq").astype(jnp.float32),
        lax.psum(part_b_out.astype(jnp.bfloat16), "seq").astype(jnp.float32),
        lax.psum(part_second_gain.astype(jnp.bfloat16), "seq").astype(jnp.float32),
        lax.psum(part_second_shift.astype(jnp.bfloat16), "seq").astype(jnp.float32),
        lax.psum(part_w_up.astype(jnp.bfloat16), "seq").astype(jnp.float32),
        lax.psum(part_b_up.astype(jnp.bfloat16), "seq").astype(jnp.float32),
        lax.psum(part_w_down.astype(jnp.bfloat16), "seq").astype(jnp.float32),
        lax.psum(part_b_down.astype(jnp.bfloat16), "seq").astype(jnp.float32),
    )
    return (
        output,
        grad_inputs,
        shard_first_gain,
        shard_first_shift,
        shard_w_query,
        shard_b_query,
        shard_w_key,
        shard_w_value,
        shard_b_value,
        shard_w_out,
        shard_b_out,
        shard_second_gain,
        shard_second_shift,
        shard_w_up,
        shard_b_up,
        shard_w_down,
        shard_b_down,
    )


def solution(mesh):
    placed = (
        P("dp", "seq", None),
        P("dp", "seq"),
        P("dp"),
        P("dp"),
        P("dp", None),
        P("dp"),
        P("dp", None),
        P("dp", None),
        P("dp"),
        P("dp", None),
        P("dp"),
        P("dp"),
        P("dp"),
        P("dp", None),
        P("dp"),
        P("dp", None),
        P("dp"),
        P("dp", "seq", None),
    )
    return jax.shard_map(
        per_device,
        mesh=mesh,
        in_specs=placed,
        out_specs=(
            P("dp", "seq", None),
            P("dp", "seq", None),
            P("dp"),
            P("dp"),
            P("dp", None),
            P("dp"),
            P("dp", None),
            P("dp", None),
            P("dp"),
            P("dp", None),
            P("dp"),
            P("dp"),
            P("dp"),
            P("dp", None),
            P("dp"),
            P("dp", None),
            P("dp"),
        ),
        check_vma=False,
    )
```

profile of v0, /device:TPU:0, one launch (start us, length us, event | category | flops | bytes accessed | tf_op | source)
XLA Modules:
  0.0 1093.1 jit_solution(9284306337476619404)
XLA Ops:
  15.2 26.3 %all-reduce.18 = (bf16[768]{0:T(1024)(128)(2,1)S(1)}, bf16[768]{0:T(1024)(128)(2,1)S(1)}, bf16[768]{0:T(1024)(128)(2,1)S(1)}, bf16[768]{0:T(1024)(128)(2,1)S(1)}...) all-reduce(bf16[768]{0:T(1024)(128)(2,1)S(1)} %dynamic-update-slice, ...), channel_id=1, replica_groups=mesh['dp'=8,'seq'=4] {'dp'}, use_global_device_ids=true, to_apply=%add.1 | all-reduce | flops 6144 | bytes 24576
  47.7 5.0 all-to-all-start
  53.4 9.6 all-gather.12.cloned.1.call-done
  70.2 16.2 %all-to-all-done = bf16[3,256,768]{1,0,2:T(4,128)(2,1)S(1)} async-done(((bf16[3,256,768]{1,0,2:T(4,128)(2,1)}), bf16[3,256,768]{1,0,2:T(4,128)(2,1)S(1)}, u32[]{:S(2)}, u32[]{:S(2)}) %all-to-all-start) | async-done | bytes 1179680 | tf_op jit(solution)/shard_map/all_to_all | solution.py:170
  86.5 4.3 all-to-all-start.2
  98.7 28.6 %all-to-all-done.2 = bf16[3,256,768]{1,0,2:T(4,128)(2,1)} async-done(((bf16[3,256,768]{1,0,2:T(4,128)(2,1)}), bf16[3,256,768]{1,0,2:T(4,128)(2,1)}, u32[]{:S(2)}, u32[]{:S(2)}) %all-to-all-start.2) | async-done | bytes 1179680 | tf_op jit(solution)/shard_map/all_to_all | solution.py:184
  127.3 4.3 all-to-all-start.1
  132.3 41.2 %all_gather.56 = s32[3,1024]{1,0:T(4,128)S(1)} all-gather(s32[3,256]{1,0:T(4,128)S(1)} %copy-done.26), channel_id=1, replica_groups=mesh['dp'=8,'seq'=4] {'seq'}, dimensions={1}, use_global_device_ids=true | all-gather | bytes 15360 | tf_op jit(solution)/shard_map/all_gather | solution.py:156
  202.1 99.2 %while.26 = (s32[]{:T(128)}, bf16[9,1024,64]{1,2,0:T(8,128)(2,1)}, f32[9,1024]{1,0:T(8,128)}, s32[9,1024]{1,0:T(8,128)}, bf16[9,1024,64]{2,1,0:T(8,128)(2,1)S(1)...) while((s32[]{:T(128)}, bf16[9,1024,64]{1,2,0:T(8,128)(2,1)}, ...), condition=%wide.region_5.6_spmd, body=%wide.region_2.5_spmd.sunk | while | flops 284228608 | bytes 30349440 | solution.py:197
  305.5 4.6 all-to-all-start.3
  311.4 10.1 all-gather
  322.1 33.6 %all-to-all-done.3 = bf16[3,1024,192]{2,0,1:T(4,128)(2,1)} async-done(((bf16[3,1024,192]{2,0,1:T(4,128)(2,1)}), bf16[3,1024,192]{2,0,1:T(4,128)(2,1)}, u32[]{:S(2)}, u32[]{:S(2)}) %all-to-all-start.3) | async-done | bytes 1179680 | tf_op jit(solution)/shard_map/all_to_all | solution.py:201
  364.3 27.2 %fusion.56 = (bf16[768,3072]{1,0:T(8,128)(2,1)}, f32[768,3072]{1,0:T(8,128)}) fusion(f32[3072]{0:T(1024)} %bitcast.275, bf16[768,3072]{1,0:T(8,128)(2,1)} %all-gather.16.cloned.1.call-done, f32[768,768]{1,0:T(8,128)S(1)} %get-tuple-element.265, f32[768]{0:T(1024)S(1)} %convert_element_type.227, f32[768]{0:T(1024)S(1)} %convert_element_type.226, ...), kind=kOutput, calls=%fused_computation.64 | convolution fusion | flops 3782541312 | bytes 21258240 | tf_op jit(solution)/shard_map/dot_general | solution.py:213
  391.5 11.6 %convert_reduce_fusion = (f32[3072]{0:T(1024)}, bf16[768,3072]{1,0:T(8,128)(2,1)S(1)}) fusion(f32[768,3072]{1,0:T(8,128)} %get-tuple-element.267, f32[3072]{0:T(1024)} %bitcast.276, bf16[768,768]{1,0:T(8,128)(2,1)} %bitcast.249, bf16[3072,768]{1,0:T(8,128)(2,1)} %all-gather.18.cloned.1.call-done), kind=kOutput, calls=%fused_computation.71 | convolution fusion | flops 3654546432 | bytes 20078592 | tf_op jit(solution)/shard_map/dot_general | solution.py:40
  403.2 4.8 multiply_reduce_fusion.1
  415.4 4.3 all-to-all-start.4
  419.8 4.5 fusion.90
  424.4 31.9 %all-to-all-done.4 = bf16[3,256,768]{1,0,2:T(4,128)(2,1)} async-done(((bf16[3,256,768]{1,0,2:T(4,128)(2,1)}), bf16[3,256,768]{1,0,2:T(4,128)(2,1)}, u32[]{:S(2)}, u32[]{:S(2)}) %all-to-all-start.4) | async-done | bytes 1179680 | tf_op jit(solution)/shard_map/all_to_all | solution.py:252
  467.1 124.2 %while.27 = (s32[]{:T(128)}, bf16[9,1024,64]{1,2,0:T(8,128)(2,1)}, bf16[9,1024,64]{1,2,0:T(8,128)(2,1)}, bf16[9,1024,64]{1,2,0:T(8,128)(2,1)}, s32[9,1024]{1,0:T...) while((s32[]{:T(128)}, bf16[9,1024,64]{1,2,0:T(8,128)(2,1)}, ...), condition=%wide.region_12.13_spmd, body=%wide.region_10.12_spmd.sunk | while | flops 681901056 | bytes 33465460 | solution.py:253
  595.3 4.4 all-to-all-start.5
  602.0 45.4 %all-to-all-done.5 = bf16[3,1024,192]{2,0,1:T(4,128)(2,1)} async-done(((bf16[3,1024,192]{2,0,1:T(4,128)(2,1)}), bf16[3,1024,192]{2,0,1:T(4,128)(2,1)}, u32[]{:S(2)}, u32[]{:S(2)}) %all-to-all-start.5) | async-done | bytes 1179680 | tf_op jit(solution)/shard_map/all_to_all | solution.py:265
  664.0 51.4 %all_to_all.120 = bf16[3,1024,192]{2,0,1:T(4,128)(2,1)S(1)} all-to-all(bf16[3,1024,192]{2,0,1:T(4,128)(2,1)} %copy.125), channel_id=1, replica_groups=mesh['dp'=8,'seq'=4] {'seq'}, dimensions={1} | all-to-all | bytes 2359296 | tf_op jit(solution)/shard_map/all_to_all | solution.py:272
  730.5 50.8 %all_to_all.121 = bf16[3,1024,192]{2,0,1:T(4,128)(2,1)S(1)} all-to-all(bf16[3,1024,192]{2,0,1:T(4,128)(2,1)} %copy.128), channel_id=1, replica_groups=mesh['dp'=8,'seq'=4] {'seq'}, dimensions={1} | all-to-all | bytes 2359296 | tf_op jit(solution)/shard_map/all_to_all | solution.py:279
  793.5 9.0 fusion.93
  802.6 10.6 fusion.102
  817.2 8.6 add_convert_fusion
  825.8 4.4 copy.135
  849.0 67.9 %reduce-scatter.15.cloned.1.call-done = f32[96,3072]{1,0:T(8,128)} async-done(((f32[768,3072]{1,0:T(8,128)}), f32[96,3072]{1,0:T(8,128)}) %reduce-scatter.15.cloned.1.call-update) | async-done | bytes 1179664 | tf_op jit(solution)/shard_map/reduce_scatter | solution.py:334
  919.0 77.7 %reduce-scatter.17.cloned.1.call-done = f32[384,768]{1,0:T(8,128)} async-done(((f32[3072,768]{1,0:T(8,128)}), f32[384,768]{1,0:T(8,128)}) %reduce-scatter.17.cloned.1.call-update) | async-done | bytes 1179664 | tf_op jit(solution)/shard_map/reduce_scatter | solution.py:336
  1005.2 26.3 %all-reduce.17 = (bf16[768]{0:T(1024)(128)(2,1)}, bf16[768]{0:T(1024)(128)(2,1)}, bf16[768]{0:T(1024)(128)(2,1)}, bf16[768]{0:T(1024)(128)(2,1)}, bf16[768]{0:T(...) all-reduce(f32[768]{0:T(1024)} %get-tuple-element.184, ...), channel_id=2, replica_groups=mesh['dp'=8,'seq'=4] {'dp'}, use_global_device_ids=true, to_apply=%region_16.17.clone | all-reduce | flops 9216 | bytes 55296
  1042.2 13.1 %all-reduce.19 = (bf16[96]{0:T(256)(128)(2,1)}, bf16[96]{0:T(256)(128)(2,1)}, bf16[96]{0:T(256)(128)(2,1)}, bf16[96]{0:T(256)(128)(2,1)}, bf16[96]{0:T(256)(128)...) all-reduce(bf16[96]{0:T(256)(128)(2,1)} %dynamic-slice.43, ...), channel_id=1, replica_groups=mesh['dp'=8,'seq'=4] {'seq'}, use_global_device_ids=true, to_apply=%region_17.18 | all-reduce | flops 1152 | bytes 4608 | tf_op jit(solution)/shard_map/psum | solution.py:356
  1070.8 8.2 all-reduce.23.cloned.1.call-done
  (398 shorter events, 429.8 us)
Async XLA Ops:
  7.2 34.9 %copy-start.1 = (bf16[3,256,768]{2,1,0:T(8,128)(2,1)S(1)}, bf16[3,256,768]{2,1,0:T(8,128)(2,1)}, u32[]{:S(2)}) copy-start(bf16[3,256,768]{2,1,0:T(8,128)(2,1)} %param.22) | copy-start | bytes 3538948
  7.3 7.0 copy-start.40
  7.3 7.3 copy-start.41
  7.3 7.5 copy-start.42
  7.3 7.7 copy-start.43
  7.3 35.4 %all-gather.8.cloned.1.call-start = ((), (), s32[]{:S(2)}) async-start(), calls=%async_computation.14 | async-start | bytes 1327104 | tf_op jit(solution)/shard_map/all_gather | solution.py:142
  8.0 54.9 %all-gather.12.cloned.1.call-start = ((), (), s32[]{:S(2)}) async-start(), calls=%async_computation.16 | async-start | bytes 1327104 | tf_op jit(solution)/shard_map/all_gather | solution.py:145
  10.3 31.3 %copy-start.18 = (f32[3,256]{1,0:T(4,128)}, f32[3,256]{1,0:T(4,128)S(1)}, u32[]{:S(2)}) copy-start(f32[3,256]{1,0:T(4,128)S(1)} %broadcast_multiply_fusion.5) | copy-start | bytes 9220
  12.1 30.6 %copy-start.19 = (f32[768]{0:T(1024)}, f32[768]{0:T(1024)S(1)}, u32[]{:S(2)}) copy-start(f32[768]{0:T(1024)S(1)} %div.35) | copy-start | bytes 9220
  47.7 38.8 %all-to-all-start = ((bf16[3,256,768]{1,0,2:T(4,128)(2,1)}), bf16[3,256,768]{1,0,2:T(4,128)(2,1)S(1)}, u32[]{:S(2)}, u32[]{:S(2)}) async-start(bf16[3,256,768]{1,0,2:T(4,128)(2,1)} %copy.100), calls=%async_computation | async-start | bytes 3145728 | tf_op jit(solution)/shard_map/all_to_all | solution.py:170
  52.6 38.8 %all-gather.10.cloned.1.call-start = ((), (), s32[]{:S(2)}) async-start(), calls=%async_computation.15 | async-start | bytes 1327104 | tf_op jit(solution)/shard_map/all_gather | solution.py:144
  86.5 40.9 %all-to-all-start.2 = ((bf16[3,256,768]{1,0,2:T(4,128)(2,1)}), bf16[3,256,768]{1,0,2:T(4,128)(2,1)}, u32[]{:S(2)}, u32[]{:S(2)}) async-start(bf16[3,256,768]{1,0,2:T(4,128)(2,1)} %copy.106), calls=%async_computation.2 | async-start | bytes 3145728 | tf_op jit(solution)/shard_map/all_to_all | solution.py:184
  90.8 270.2 %all-gather.14.cloned.1.call-start = ((), (), s32[]{:S(2)}) async-start(), calls=%async_computation.17 | async-start | bytes 1327104 | tf_op jit(solution)/shard_map/all_gather | solution.py:147
  98.7 33.6 %copy-start.26 = (s32[3,256]{1,0:T(4,128)S(1)}, s32[3,256]{1,0:T(4,128)}, u32[]{:S(2)}) copy-start(s32[3,256]{1,0:T(4,128)} %param.23) | copy-start | bytes 9220
  127.3 63.0 %all-to-all-start.1 = ((bf16[3,256,768]{1,0,2:T(4,128)(2,1)}), bf16[3,256,768]{1,0,2:T(4,128)(2,1)}, u32[]{:S(2)}, u32[]{:S(2)}) async-start(bf16[3,256,768]{1,0,2:T(4,128)(2,1)} %copy.103), calls=%async_computation.1 | async-start | bytes 3145728 | tf_op jit(solution)/shard_map/all_to_all | solution.py:177
  131.7 232.6 %all-gather.16.cloned.1.call-start = ((), (), s32[]{:S(2)}) async-start(), calls=%async_computation.18 | async-start | bytes 5308416 | tf_op jit(solution)/shard_map/all_gather | solution.py:151
  305.5 50.2 %all-to-all-start.3 = ((bf16[3,1024,192]{2,0,1:T(4,128)(2,1)}), bf16[3,1024,192]{2,0,1:T(4,128)(2,1)}, u32[]{:S(2)}, u32[]{:S(2)}) async-start(bf16[3,1024,192]{2,0,1:T(4,128)(2,1)} %copy.112), calls=%async_computation.3 | async-start | bytes 4194304 | tf_op jit(solution)/shard_map/all_to_all | solution.py:201
  310.1 81.4 %all-gather.18.cloned.1.call-start = ((), (), s32[]{:S(2)}) async-start(), calls=%async_computation.19 | async-start | bytes 5308416 | tf_op jit(solution)/shard_map/all_gather | solution.py:153
  391.5 11.6 %copy-start.32 = (bf16[768,3072]{1,0:T(8,128)(2,1)S(1)}, bf16[768,3072]{1,0:T(8,128)(2,1)}, u32[]{:S(2)}) copy-start(bf16[768,3072]{1,0:T(8,128)(2,1)} %all-gather.16.cloned.1.call-done) | copy-start | bytes 14155780
  415.4 40.9 %all-to-all-start.4 = ((bf16[3,256,768]{1,0,2:T(4,128)(2,1)}), bf16[3,256,768]{1,0,2:T(4,128)(2,1)}, u32[]{:S(2)}, u32[]{:S(2)}) async-start(bf16[3,256,768]{1,0,2:T(4,128)(2,1)} %copy.115), calls=%async_computation.4 | async-start | bytes 3145728 | tf_op jit(solution)/shard_map/all_to_all | solution.py:252
  419.8 418.5 %reduce-scatter.13.cloned.1.call-start = ((), (), s32[]{:S(2)}) async-start(), calls=%async_computation.23 | async-start | bytes 2654208 | tf_op jit(solution)/shard_map/reduce_scatter | solution.py:330
  595.3 52.1 %all-to-all-start.5 = ((bf16[3,1024,192]{2,0,1:T(4,128)(2,1)}), bf16[3,1024,192]{2,0,1:T(4,128)(2,1)}, u32[]{:S(2)}, u32[]{:S(2)}) async-start(bf16[3,1024,192]{2,0,1:T(4,128)(2,1)} %copy.122), calls=%async_computation.5 | async-start | bytes 4194304 | tf_op jit(solution)/shard_map/all_to_all | solution.py:265
  599.8 244.3 %reduce-scatter.7.cloned.1.call-start = ((), (), s32[]{:S(2)}) async-start(), calls=%async_computation.20 | async-start | bytes 2654208 | tf_op jit(solution)/shard_map/reduce_scatter | solution.py:325
  659.9 185.7 %reduce-scatter.9.cloned.1.call-start = ((), (), s32[]{:S(2)}) async-start(), calls=%async_computation.21 | async-start | bytes 2654208 | tf_op jit(solution)/shard_map/reduce_scatter | solution.py:327
  726.4 120.9 %reduce-scatter.11.cloned.1.call-start = ((), (), s32[]{:S(2)}) async-start(), calls=%async_computation.22 | async-start | bytes 2654208 | tf_op jit(solution)/shard_map/reduce_scatter | solution.py:328
  793.5 123.4 %reduce-scatter.15.cloned.1.call-start = ((), (), s32[]{:S(2)}) async-start(), calls=%async_computation.24 | async-start | bytes 10616832 | tf_op jit(solution)/shard_map/reduce_scatter | solution.py:334
  802.5 194.2 %reduce-scatter.17.cloned.1.call-start = ((), (), s32[]{:S(2)}) async-start(), calls=%async_computation.25 | async-start | bytes 10616832 | tf_op jit(solution)/shard_map/reduce_scatter | solution.py:336
  813.2 265.8 %all-reduce.23.cloned.1.call-start = ((), (), s32[]{:S(2)}) async-start(), calls=%async_computation.26 | async-start | bytes 3538944 | tf_op jit(solution)/shard_map/psum | solution.py:358
  825.8 7.0 copy-start.3
  849.0 149.9 %copy-start.10 = (bf16[768,768]{1,0:T(8,128)(2,1)S(1)}, bf16[768,768]{1,0:T(8,128)(2,1)}, u32[]{:S(2)}) copy-start(bf16[768,768]{1,0:T(8,128)(2,1)} %reshape.310) | copy-start | bytes 3538948
  849.0 149.9 %copy-start.34 = (bf16[768,768]{1,0:T(8,128)(2,1)S(1)}, bf16[768,768]{1,0:T(8,128)(2,1)}, u32[]{:S(2)}) copy-start(bf16[768,768]{1,0:T(8,128)(2,1)} %all-gather.10.cloned.1.call-done) | copy-start | bytes 3538948
  1001.3 65.9 %copy-start.6 = (f32[768,768]{1,0:T(8,128)S(1)}, f32[768,768]{1,0:T(8,128)}, u32[]{:S(2)}) copy-start(f32[768,768]{1,0:T(8,128)} %copy-done.5) | copy-start | bytes 7077892
  (40 other events, 126.2 us)
Sparse Core Ops, SparseCore 0:
  10.0 26.8 all-gather.7
  38.8 24.0 all-gather.11
  64.8 24.0 all-gather.9
  93.2 26.1 all-gather.13
  134.1 41.8 all-gather.15
  312.5 41.8 all-gather.17
  424.5 45.4 reduce-scatter.12
  660.0 43.1 reduce-scatter.6
  726.5 43.1 reduce-scatter.8
  793.6 43.2 reduce-scatter.10
  840.4 76.4 reduce-scatter.14
  920.2 76.4 reduce-scatter.16
  1000.7 78.2 all-reduce.22
where the time goes:
time: 1110 us; the launch traced here: 1090 us
  waiting for transfers between devices  323 us (29%)
  matrix products  266 us (24%)
  blocking collectives  219 us (20%)
  local copies, waits for them, and re-layouts  172 us (15%)
  other arithmetic  68 us (6%)
  starting transfers between devices  27.7 us (2%)
  between operations  16.7 us (2%)
    reduce_scatter x1, waiting for transfers between devices, per_device(): lax.psum_scatter(d_w_down, 'dp', scatter_dimension=0, tiled=True)  77.7 us
    reduce_scatter x1, waiting for transfers between devices, per_device(): lax.psum_scatter(d_w_up, 'dp', scatter_dimension=0, tiled=True)  67.9 us
    unnamed x2, blocking collectives  52.5 us
    all_to_all x1, blocking collectives, per_device(): lax.all_to_all(from_pairs(grad_key_pairs, seqs_here, heads_here), 'seq',...  51.4 us
    all_to_all x1, blocking collectives, per_device(): lax.all_to_all(from_pairs(grad_value_pairs, seqs_here, heads_here), 'seq'...  50.8 us
    all_to_all x1, waiting for transfers between devices, per_device(): lax.all_to_all(from_pairs(grad_query_pairs, seqs_here, heads_here), 'seq'...  45.4 us
    all_gather x1, blocking collectives, per_device(): full_segments = lax.all_gather(segment_ids, 'seq', axis=1, tiled=True)  41.2 us
    dot_general x18, matrix products, masked_scores(): jnp.einsum('qd,kd->qk', query_pair, key_pair, preferred_element_type=jnp....  38.3 us
  transfers between devices with their start and end apart: 19, of which 9 were waited for; matrix products, arithmetic and copies ran while one was open for 41% of the time, Pallas kernels for 0%

commit v1 on v0

--- a/solution.py
+++ b/solution.py
@@ -198,9 +198,10 @@
         attend_forward, (query_pairs, key_pairs, value_pairs, segment_pairs)
     )
     attn_heads = from_pairs(attn_pairs, seqs_here, heads_here)
-    attn_tok = lax.all_to_all(attn_heads, "seq", split_axis=1, concat_axis=2, tiled=True).reshape(
-        token_rows, model_width
-    )
+    attn_tok = jnp.concatenate(
+        lax.all_to_all(jnp.stack(jnp.split(attn_heads, lax.axis_size("seq"), axis=1)), "seq", 0, 0),
+        axis=2,
+    ).reshape(token_rows, model_width)
     middle = (
         flat_in
         + jnp.dot(attn_tok, w_out, preferred_element_type=jnp.float32)

time: 1110 us -> 1090 us (0.982)
  waiting for transfers between devices: 323 us -> 304 us
    all_to_all x1, waiting for transfers between devices: 33.6 us -> 14.2 us  [per_device(): lax.all_to_all(jnp.stack(jnp.split(attn_heads, lax.axis_size('seq'), axis...]
  transfers between devices with their start and end apart: 19 -> 19, of which waited for: 9 -> 9; matrix products, arithmetic and copies ran while one was open for 41% -> 42% of each run, Pallas kernels for 0% -> 0%
where the time goes in v1:
time: 1090 us; the launch traced here: 1070 us
  waiting for transfers between devices  304 us (28%)
  matrix products  266 us (24%)
  blocking collectives  219 us (20%)
  local copies, waits for them, and re-layouts  171 us (16%)
  other arithmetic  69.1 us (6%)
  starting transfers between devices  26.8 us (2%)
  between operations  16.9 us (2%)
    reduce_scatter x1, waiting for transfers between devices, per_device(): lax.psum_scatter(d_w_down, 'dp', scatter_dimension=0, tiled=True)  77.7 us
    reduce_scatter x1, waiting for transfers between devices, per_device(): lax.psum_scatter(d_w_up, 'dp', scatter_dimension=0, tiled=True)  67.7 us
    unnamed x2, blocking collectives  52.5 us
    all_to_all x1, blocking collectives, per_device(): lax.all_to_all(from_pairs(grad_key_pairs, seqs_here, heads_here), 'seq',...  51.5 us
    all_to_all x1, blocking collectives, per_device(): lax.all_to_all(from_pairs(grad_value_pairs, seqs_here, heads_here), 'seq'...  50.8 us
    all_to_all x1, waiting for transfers between devices, per_device(): lax.all_to_all(from_pairs(grad_query_pairs, seqs_here, heads_here), 'seq'...  45.5 us
    all_gather x1, blocking collectives, per_device(): full_segments = lax.all_gather(segment_ids, 'seq', axis=1, tiled=True)  41.2 us
    dot_general x18, matrix products, masked_scores(): jnp.einsum('qd,kd->qk', query_pair, key_pair, preferred_element_type=jnp....  38.3 us
  transfers between devices with their start and end apart: 19, of which 9 were waited for; matrix products, arithmetic and copies ran while one was open for 42% of the time, Pallas kernels for 0%

profile of v1, /device:TPU:0, one launch (start us, length us, event | category | flops | bytes accessed | tf_op | source)
XLA Modules:
  0.0 1073.0 jit_solution(4321748159664221893)
XLA Ops:
  15.2 26.3 %all-reduce.18 = (bf16[768]{0:T(1024)(128)(2,1)S(1)}, bf16[768]{0:T(1024)(128)(2,1)S(1)}, bf16[768]{0:T(1024)(128)(2,1)S(1)}, bf16[768]{0:T(1024)(128)(2,1)S(1)}...) all-reduce(bf16[768]{0:T(1024)(128)(2,1)S(1)} %dynamic-update-slice, ...), channel_id=1, replica_groups=mesh['dp'=8,'seq'=4] {'dp'}, use_global_device_ids=true, to_apply=%add.1 | all-reduce | flops 6144 | bytes 24576
  47.7 5.0 all-to-all-start
  53.4 9.6 all-gather.12.cloned.1.call-done
  70.2 16.2 %all-to-all-done = bf16[3,256,768]{1,0,2:T(4,128)(2,1)S(1)} async-done(((bf16[3,256,768]{1,0,2:T(4,128)(2,1)}), bf16[3,256,768]{1,0,2:T(4,128)(2,1)S(1)}, u32[]{:S(2)}, u32[]{:S(2)}) %all-to-all-start) | async-done | bytes 1179680 | tf_op jit(solution)/shard_map/all_to_all | solution.py:170
  86.5 4.3 all-to-all-start.2
  98.7 28.6 %all-to-all-done.2 = bf16[3,256,768]{1,0,2:T(4,128)(2,1)} async-done(((bf16[3,256,768]{1,0,2:T(4,128)(2,1)}), bf16[3,256,768]{1,0,2:T(4,128)(2,1)}, u32[]{:S(2)}, u32[]{:S(2)}) %all-to-all-start.2) | async-done | bytes 1179680 | tf_op jit(solution)/shard_map/all_to_all | solution.py:184
  127.3 4.3 all-to-all-start.1
  132.3 41.2 %all_gather.56 = s32[3,1024]{1,0:T(4,128)S(1)} all-gather(s32[3,256]{1,0:T(4,128)S(1)} %copy-done.27), channel_id=1, replica_groups=mesh['dp'=8,'seq'=4] {'seq'}, dimensions={1}, use_global_device_ids=true | all-gather | bytes 15360 | tf_op jit(solution)/shard_map/all_gather | solution.py:156
  202.1 99.2 %while.26 = (s32[]{:T(128)}, bf16[9,1024,64]{1,2,0:T(8,128)(2,1)}, f32[9,1024]{1,0:T(8,128)}, s32[9,1024]{1,0:T(8,128)}, bf16[9,1024,64]{2,1,0:T(8,128)(2,1)S(1)...) while((s32[]{:T(128)}, bf16[9,1024,64]{1,2,0:T(8,128)(2,1)}, ...), condition=%wide.region_5.6_spmd, body=%wide.region_2.5_spmd.sunk | while | flops 284228608 | bytes 30349440 | solution.py:197
  309.7 10.1 all-gather
  320.4 14.2 %all-to-all-done.3 = bf16[4,3,256,192]{2,3,1,0:T(8,128)(2,1)S(1)} async-done(((bf16[4,3,256,192]{2,3,1,0:T(8,128)(2,1)}), bf16[4,3,256,192]{2,3,1,0:T(8,128)(2,1)S(1)}, u32[]{:S(2)}, u32[]{:S(2)}) %all-to-all-start.3) | async-done | bytes 1179680 | tf_op jit(solution)/shard_map/all_to_all | solution.py:202
  343.9 27.3 %fusion.56 = (bf16[768,3072]{1,0:T(8,128)(2,1)}, f32[768,3072]{1,0:T(8,128)}) fusion(f32[3072]{0:T(1024)} %bitcast.281, bf16[768,3072]{1,0:T(8,128)(2,1)} %all-gather.16.cloned.1.call-done, f32[768,768]{1,0:T(8,128)S(1)} %get-tuple-element.269, f32[768]{0:T(1024)S(1)} %convert_element_type.227, f32[768]{0:T(1024)S(1)} %convert_element_type.226, ...), kind=kOutput, calls=%fused_computation.64 | convolution fusion | flops 3782541312 | bytes 21258240 | tf_op jit(solution)/shard_map/dot_general | solution.py:214
  371.2 11.9 %convert_reduce_fusion = (f32[3072]{0:T(1024)}, bf16[768,3072]{1,0:T(8,128)(2,1)S(1)}) fusion(f32[768,3072]{1,0:T(8,128)} %get-tuple-element.271, f32[3072]{0:T(1024)} %bitcast.282, bf16[768,768]{1,0:T(8,128)(2,1)} %bitcast.254, bf16[3072,768]{1,0:T(8,128)(2,1)} %all-gather.18.cloned.1.call-done), kind=kOutput, calls=%fused_computation.71 | convolution fusion | flops 3654546432 | bytes 20078592 | tf_op jit(solution)/shard_map/dot_general | solution.py:40
  383.1 4.8 multiply_reduce_fusion.1
  395.3 4.4 all-to-all-start.4
  399.8 4.5 fusion.90
  404.3 31.9 %all-to-all-done.4 = bf16[3,256,768]{1,0,2:T(4,128)(2,1)} async-done(((bf16[3,256,768]{1,0,2:T(4,128)(2,1)}), bf16[3,256,768]{1,0,2:T(4,128)(2,1)}, u32[]{:S(2)}, u32[]{:S(2)}) %all-to-all-start.4) | async-done | bytes 1179680 | tf_op jit(solution)/shard_map/all_to_all | solution.py:253
  446.8 124.2 %while.27 = (s32[]{:T(128)}, bf16[9,1024,64]{1,2,0:T(8,128)(2,1)}, bf16[9,1024,64]{1,2,0:T(8,128)(2,1)}, bf16[9,1024,64]{1,2,0:T(8,128)(2,1)}, s32[9,1024]{1,0:T...) while((s32[]{:T(128)}, bf16[9,1024,64]{1,2,0:T(8,128)(2,1)}, ...), condition=%wide.region_12.13_spmd, body=%wide.region_10.12_spmd.sunk | while | flops 681901056 | bytes 33465460 | solution.py:254
  575.1 4.4 all-to-all-start.5
  581.8 45.5 %all-to-all-done.5 = bf16[3,1024,192]{2,0,1:T(4,128)(2,1)} async-done(((bf16[3,1024,192]{2,0,1:T(4,128)(2,1)}), bf16[3,1024,192]{2,0,1:T(4,128)(2,1)}, u32[]{:S(2)}, u32[]{:S(2)}) %all-to-all-start.5) | async-done | bytes 1179680 | tf_op jit(solution)/shard_map/all_to_all | solution.py:266
  627.2 4.2 copy.124
  643.8 51.5 %all_to_all.110 = bf16[3,1024,192]{2,0,1:T(4,128)(2,1)S(1)} all-to-all(bf16[3,1024,192]{2,0,1:T(4,128)(2,1)} %copy.125), channel_id=1, replica_groups=mesh['dp'=8,'seq'=4] {'seq'}, dimensions={1} | all-to-all | bytes 2359296 | tf_op jit(solution)/shard_map/all_to_all | solution.py:273
  710.3 50.8 %all_to_all.111 = bf16[3,1024,192]{2,0,1:T(4,128)(2,1)S(1)} all-to-all(bf16[3,1024,192]{2,0,1:T(4,128)(2,1)} %copy.128), channel_id=1, replica_groups=mesh['dp'=8,'seq'=4] {'seq'}, dimensions={1} | all-to-all | bytes 2359296 | tf_op jit(solution)/shard_map/all_to_all | solution.py:280
  773.4 9.0 fusion.93
  782.4 10.6 fusion.102
  797.0 8.6 add_convert_fusion
  805.6 4.4 copy.133
  828.8 67.7 %reduce-scatter.15.cloned.1.call-done = f32[96,3072]{1,0:T(8,128)} async-done(((f32[768,3072]{1,0:T(8,128)}), f32[96,3072]{1,0:T(8,128)}) %reduce-scatter.15.cloned.1.call-update) | async-done | bytes 1179664 | tf_op jit(solution)/shard_map/reduce_scatter | solution.py:335
  898.7 77.7 %reduce-scatter.17.cloned.1.call-done = f32[384,768]{1,0:T(8,128)} async-done(((f32[3072,768]{1,0:T(8,128)}), f32[384,768]{1,0:T(8,128)}) %reduce-scatter.17.cloned.1.call-update) | async-done | bytes 1179664 | tf_op jit(solution)/shard_map/reduce_scatter | solution.py:337
  984.9 26.2 %all-reduce.17 = (bf16[768]{0:T(1024)(128)(2,1)}, bf16[768]{0:T(1024)(128)(2,1)}, bf16[768]{0:T(1024)(128)(2,1)}, bf16[768]{0:T(1024)(128)(2,1)}, bf16[768]{0:T(...) all-reduce(f32[768]{0:T(1024)} %get-tuple-element.184, ...), channel_id=2, replica_groups=mesh['dp'=8,'seq'=4] {'dp'}, use_global_device_ids=true, to_apply=%region_16.17.clone | all-reduce | flops 9216 | bytes 55296
  1021.8 13.1 %all-reduce.19 = (bf16[96]{0:T(256)(128)(2,1)}, bf16[96]{0:T(256)(128)(2,1)}, bf16[96]{0:T(256)(128)(2,1)}, bf16[96]{0:T(256)(128)(2,1)}, bf16[96]{0:T(256)(128)...) all-reduce(bf16[96]{0:T(256)(128)(2,1)} %dynamic-slice.43, ...), channel_id=1, replica_groups=mesh['dp'=8,'seq'=4] {'seq'}, use_global_device_ids=true, to_apply=%region_17.18 | all-reduce | flops 1152 | bytes 4608 | tf_op jit(solution)/shard_map/psum | solution.py:357
  1050.3 8.3 all-reduce.23.cloned.1.call-done
  (401 shorter events, 428.7 us)
Async XLA Ops:
  7.2 34.9 %copy-start.1 = (bf16[3,256,768]{2,1,0:T(8,128)(2,1)S(1)}, bf16[3,256,768]{2,1,0:T(8,128)(2,1)}, u32[]{:S(2)}) copy-start(bf16[3,256,768]{2,1,0:T(8,128)(2,1)} %param.22) | copy-start | bytes 3538948
  7.3 7.0 copy-start.41
  7.3 7.3 copy-start.42
  7.3 7.5 copy-start.43
  7.3 7.7 copy-start.44
  7.3 35.4 %all-gather.8.cloned.1.call-start = ((), (), s32[]{:S(2)}) async-start(), calls=%async_computation.14 | async-start | bytes 1327104 | tf_op jit(solution)/shard_map/all_gather | solution.py:142
  8.0 54.9 %all-gather.12.cloned.1.call-start = ((), (), s32[]{:S(2)}) async-start(), calls=%async_computation.16 | async-start | bytes 1327104 | tf_op jit(solution)/shard_map/all_gather | solution.py:145
  10.3 31.3 %copy-start.19 = (f32[3,256]{1,0:T(4,128)}, f32[3,256]{1,0:T(4,128)S(1)}, u32[]{:S(2)}) copy-start(f32[3,256]{1,0:T(4,128)S(1)} %broadcast_multiply_fusion.5) | copy-start | bytes 9220
  12.1 30.6 %copy-start.20 = (f32[768]{0:T(1024)}, f32[768]{0:T(1024)S(1)}, u32[]{:S(2)}) copy-start(f32[768]{0:T(1024)S(1)} %div.35) | copy-start | bytes 9220
  47.7 38.8 %all-to-all-start = ((bf16[3,256,768]{1,0,2:T(4,128)(2,1)}), bf16[3,256,768]{1,0,2:T(4,128)(2,1)S(1)}, u32[]{:S(2)}, u32[]{:S(2)}) async-start(bf16[3,256,768]{1,0,2:T(4,128)(2,1)} %copy.102), calls=%async_computation | async-start | bytes 3145728 | tf_op jit(solution)/shard_map/all_to_all | solution.py:170
  52.6 38.8 %all-gather.10.cloned.1.call-start = ((), (), s32[]{:S(2)}) async-start(), calls=%async_computation.15 | async-start | bytes 1327104 | tf_op jit(solution)/shard_map/all_gather | solution.py:144
  86.5 40.9 %all-to-all-start.2 = ((bf16[3,256,768]{1,0,2:T(4,128)(2,1)}), bf16[3,256,768]{1,0,2:T(4,128)(2,1)}, u32[]{:S(2)}, u32[]{:S(2)}) async-start(bf16[3,256,768]{1,0,2:T(4,128)(2,1)} %copy.108), calls=%async_computation.2 | async-start | bytes 3145728 | tf_op jit(solution)/shard_map/all_to_all | solution.py:184
  90.8 249.9 %all-gather.14.cloned.1.call-start = ((), (), s32[]{:S(2)}) async-start(), calls=%async_computation.17 | async-start | bytes 1327104 | tf_op jit(solution)/shard_map/all_gather | solution.py:147
  98.7 33.6 %copy-start.27 = (s32[3,256]{1,0:T(4,128)S(1)}, s32[3,256]{1,0:T(4,128)}, u32[]{:S(2)}) copy-start(s32[3,256]{1,0:T(4,128)} %param.23) | copy-start | bytes 9220
  127.3 63.0 %all-to-all-start.1 = ((bf16[3,256,768]{1,0,2:T(4,128)(2,1)}), bf16[3,256,768]{1,0,2:T(4,128)(2,1)}, u32[]{:S(2)}, u32[]{:S(2)}) async-start(bf16[3,256,768]{1,0,2:T(4,128)(2,1)} %copy.105), calls=%async_computation.1 | async-start | bytes 3145728 | tf_op jit(solution)/shard_map/all_to_all | solution.py:177
  131.7 212.3 %all-gather.16.cloned.1.call-start = ((), (), s32[]{:S(2)}) async-start(), calls=%async_computation.18 | async-start | bytes 5308416 | tf_op jit(solution)/shard_map/all_gather | solution.py:151
  304.7 30.0 %all-to-all-start.3 = ((bf16[4,3,256,192]{2,3,1,0:T(8,128)(2,1)}), bf16[4,3,256,192]{2,3,1,0:T(8,128)(2,1)S(1)}, u32[]{:S(2)}, u32[]{:S(2)}) async-start(bf16[4,3,256,192]{2,3,1,0:T(8,128)(2,1)} %pad_maximum_fusion), calls=%async_computation.3 | async-start | bytes 2359296 | tf_op jit(solution)/shard_map/all_to_all | solution.py:202
  308.4 62.9 %all-gather.18.cloned.1.call-start = ((), (), s32[]{:S(2)}) async-start(), calls=%async_computation.19 | async-start | bytes 5308416 | tf_op jit(solution)/shard_map/all_gather | solution.py:153
  371.2 11.9 %copy-start.33 = (bf16[768,3072]{1,0:T(8,128)(2,1)S(1)}, bf16[768,3072]{1,0:T(8,128)(2,1)}, u32[]{:S(2)}) copy-start(bf16[768,3072]{1,0:T(8,128)(2,1)} %all-gather.16.cloned.1.call-done) | copy-start | bytes 14155780
  395.3 40.9 %all-to-all-start.4 = ((bf16[3,256,768]{1,0,2:T(4,128)(2,1)}), bf16[3,256,768]{1,0,2:T(4,128)(2,1)}, u32[]{:S(2)}, u32[]{:S(2)}) async-start(bf16[3,256,768]{1,0,2:T(4,128)(2,1)} %copy.115), calls=%async_computation.4 | async-start | bytes 3145728 | tf_op jit(solution)/shard_map/all_to_all | solution.py:253
  399.7 418.4 %reduce-scatter.13.cloned.1.call-start = ((), (), s32[]{:S(2)}) async-start(), calls=%async_computation.23 | async-start | bytes 2654208 | tf_op jit(solution)/shard_map/reduce_scatter | solution.py:331
  575.1 52.2 %all-to-all-start.5 = ((bf16[3,1024,192]{2,0,1:T(4,128)(2,1)}), bf16[3,1024,192]{2,0,1:T(4,128)(2,1)}, u32[]{:S(2)}, u32[]{:S(2)}) async-start(bf16[3,1024,192]{2,0,1:T(4,128)(2,1)} %copy.122), calls=%async_computation.5 | async-start | bytes 4194304 | tf_op jit(solution)/shard_map/all_to_all | solution.py:266
  579.5 244.3 %reduce-scatter.7.cloned.1.call-start = ((), (), s32[]{:S(2)}) async-start(), calls=%async_computation.20 | async-start | bytes 2654208 | tf_op jit(solution)/shard_map/reduce_scatter | solution.py:326
  639.7 185.8 %reduce-scatter.9.cloned.1.call-start = ((), (), s32[]{:S(2)}) async-start(), calls=%async_computation.21 | async-start | bytes 2654208 | tf_op jit(solution)/shard_map/reduce_scatter | solution.py:328
  706.2 120.9 %reduce-scatter.11.cloned.1.call-start = ((), (), s32[]{:S(2)}) async-start(), calls=%async_computation.22 | async-start | bytes 2654208 | tf_op jit(solution)/shard_map/reduce_scatter | solution.py:329
  773.3 123.3 %reduce-scatter.15.cloned.1.call-start = ((), (), s32[]{:S(2)}) async-start(), calls=%async_computation.24 | async-start | bytes 10616832 | tf_op jit(solution)/shard_map/reduce_scatter | solution.py:335
  782.4 194.0 %reduce-scatter.17.cloned.1.call-start = ((), (), s32[]{:S(2)}) async-start(), calls=%async_computation.25 | async-start | bytes 10616832 | tf_op jit(solution)/shard_map/reduce_scatter | solution.py:337
  793.0 265.7 %all-reduce.23.cloned.1.call-start = ((), (), s32[]{:S(2)}) async-start(), calls=%async_computation.26 | async-start | bytes 3538944 | tf_op jit(solution)/shard_map/psum | solution.py:359
  805.6 7.0 copy-start.3
  828.8 149.8 %copy-start.11 = (bf16[768,768]{1,0:T(8,128)(2,1)S(1)}, bf16[768,768]{1,0:T(8,128)(2,1)}, u32[]{:S(2)}) copy-start(bf16[768,768]{1,0:T(8,128)(2,1)} %reshape.309) | copy-start | bytes 3538948
  828.8 149.8 %copy-start.35 = (bf16[768,768]{1,0:T(8,128)(2,1)S(1)}, bf16[768,768]{1,0:T(8,128)(2,1)}, u32[]{:S(2)}) copy-start(bf16[768,768]{1,0:T(8,128)(2,1)} %all-gather.10.cloned.1.call-done) | copy-start | bytes 3538948
  981.0 65.8 %copy-start.6 = (f32[768,768]{1,0:T(8,128)S(1)}, f32[768,768]{1,0:T(8,128)}, u32[]{:S(2)}) copy-start(f32[768,768]{1,0:T(8,128)} %copy-done.5) | copy-start | bytes 7077892
  (41 other events, 127.1 us)
Sparse Core Ops, SparseCore 0:
  10.0 26.8 all-gather.7
  38.8 24.0 all-gather.11
  64.8 24.0 all-gather.9
  93.2 26.1 all-gather.13
  134.1 41.7 all-gather.15
  310.8 41.9 all-gather.17
  404.5 45.2 reduce-scatter.12
  639.8 43.0 reduce-scatter.6
  706.3 43.0 reduce-scatter.8
  773.4 43.0 reduce-scatter.10
  820.0 76.4 reduce-scatter.14
  899.9 76.4 reduce-scatter.16
  980.4 78.1 all-reduce.22
